TPU v7x, 512 devices: a whole 4x4x16 slice. The times are simulated.
512 devices in a mesh: grp: 32 (over z, x_lo), ep: 16 (over y, x_hi, core).
Axes of the slice: x: 4 (x_hi: 2, x_lo: 2; x = x_hi * 2 + x_lo), y: 4, z: 16, core: 2. Of those that a mesh axis runs over, the one named last changes fastest.
Arguments:
- hidden: bfloat16 [256, 1536], P('grp', 'ep'), may hold values from -12 to 12
- query: bfloat16 [256, 1536], P('grp'), may hold values from -16 to 16
- new_kv: bfloat16 [256, 2, 512], P('grp'), may hold values from -4 to 4
- key_cache: bfloat16 [98304, 512], P(('grp', 'ep')), may hold values from -6 to 6
- value_cache: bfloat16 [98304, 512], P(('grp', 'ep')), may hold values from -4 to 4
- page_owner: int32 [6144], P(('grp', 'ep')), may hold values from 0 to 15, as said below
- page_fill: int32 [6144], P(('grp', 'ep')), may hold values from 1 to 16, as said below
- out_weight: bfloat16 [1536, 1536], P('grp', 'ep'), may hold values from -0.75 to 0.75
- norm_gain: float32 [1536], P('ep'), may hold values from 0.25 to 1.75
- gate_up: bfloat16 [32, 1536, 1024], P('grp'), may hold values from -0.15625 to 0.15625
- down: bfloat16 [32, 512, 1536], P('grp'), may hold values from -0.25 to 0.25
- routes: int32 [256, 8], P('grp'), may hold values from 0 to 31, all different within a row; in each aligned block of 8 rows (0 to 7, 8 to 15, ...) at most 4 rows name the same one
- route_weight: bfloat16 [256, 8], P('grp'), may hold values from 0.049804688 to 0.3984375
Outputs:
- layer_out: bfloat16 [256, 1536], P('grp', 'ep')
- attn_out: bfloat16 [256, 1536], P('grp')
Inputs may be any that keep to these rules, and one draw needn't show every extreme that they name: `routes`: each row names 8 different experts. In each group's 8 rows (aligned blocks of 8 rows) no expert is named by more than 4 rows, a bound that some block reaches. `page_owner`: A value r under 8 names row r of the page's own group; a value 8 + r names row r of the partner group, whose index differs in the lowest bit. The first page_fill[p] tokens of page p are cached; the rest of the page is unused. The first page of every device is full.
All inputs are finite; a program needn't handle non-finite values.
Results may differ from a plain program's by a relative error of at most 0.017.
Values may be sent and summed in bfloat16 or wider, within the bound.
A program may use at most 64 MiB of HBM per device.

v0:
```python
import jax
import jax.numpy as jnp
from jax import lax
from jax.sharding import PartitionSpec as P

D = 1536
HEADS = 24
KV_HEADS = 8
HD = 64
FF = 512
TOP = 8
masked_score = -1e30
norm_epsilon = 1e-05


def from_partner(block, axis, apart):
    count = lax.axis_size(axis)
    route = []
    for low in range(count):
        high = low | 1 << apart
        if high != low and high < count:
            route += [(low, high), (high, low)]
    return lax.ppermute(block, axis, route)


def combined_all(part, axis, combine):
    gathered = jax.tree.map(lambda a: lax.all_gather(a, axis), part)

    def take(source):
        return jax.tree.map(lambda a: lax.dynamic_index_in_dim(a, source, 0, False), gathered)

    return lax.fori_loop(
        1, lax.axis_size(axis), lambda source, state: combine(state, take(source)), take(0)
    )


def merge_stack(parts):
    maxes, totals, accums = parts
    highest = jnp.max(maxes, 0)
    factors = jnp.exp(maxes - highest[None])
    return (highest, jnp.sum(totals * factors, 0), jnp.sum(accums * factors[..., None], 0))


def merge_parts(earlier, later):
    max_one, total_one, accum_one = earlier
    max_two, total_two, accum_two = later
    highest = jnp.maximum(max_one, max_two)
    factor_one = jnp.exp(max_one - highest)
    factor_two = jnp.exp(max_two - highest)
    return (
        highest,
        total_one * factor_one + total_two * factor_two,
        accum_one * factor_one[..., None] + accum_two * factor_two[..., None],
    )


def per_device(
    hidden,
    query,
    new_kv,
    key_cache,
    value_cache,
    page_owner,
    page_fill,
    out_weight,
    norm_gain,
    gate_up,
    down,
    routes,
    route_weight,
):
    row_count = query.shape[0]
    group_count = lax.axis_size("grp")
    head_group = HEADS // KV_HEADS
    page_count = page_owner.shape[0]
    token_count = key_cache.shape[0]
    page_length = token_count // page_count
    both_rows = 2 * row_count
    scale = HD ** (-0.5)
    partner_query = from_partner(query, "grp", 0)
    all_queries = jnp.concatenate([query, partner_query], 0)
    query_heads = (
        all_queries.reshape(both_rows, KV_HEADS, head_group, HD)
        .transpose(1, 0, 2, 3)
        .reshape(KV_HEADS, both_rows * head_group, HD)
    )
    key_heads = key_cache.reshape(token_count, KV_HEADS, HD)
    value_heads = value_cache.reshape(token_count, KV_HEADS, HD)
    scores = (
        jnp.einsum("kqd,tkd->kqt", query_heads, key_heads, preferred_element_type=jnp.float32)
        * scale
    )
    scores = scores.reshape(KV_HEADS, both_rows, head_group, token_count)
    row_index = jnp.arange(both_rows, dtype=jnp.int32)
    in_page = jnp.arange(page_length, dtype=jnp.int32)
    usable = (page_owner[None, :, None] == row_index[:, None, None]) & (
        in_page[None, None, :] < page_fill[None, :, None]
    )
    usable = usable.reshape(both_rows, token_count)[None, :, None, :]
    local_top = jnp.max(jnp.where(usable, scores, masked_score), -1)
    weights = jnp.where(usable, jnp.exp(scores - local_top[..., None]), 0.0)
    local_total = jnp.sum(weights, -1)
    rounded = weights.astype(jnp.bfloat16).reshape(KV_HEADS, both_rows * head_group, token_count)
    local_accum = jnp.einsum(
        "kqt,tkd->kqd", rounded, value_heads, preferred_element_type=jnp.float32
    )
    part_max = local_top.transpose(1, 0, 2).reshape(both_rows, HEADS)
    part_total = local_total.transpose(1, 0, 2).reshape(both_rows, HEADS)
    part_accum = (
        local_accum.reshape(KV_HEADS, both_rows, head_group, HD)
        .transpose(1, 0, 2, 3)
        .reshape(both_rows, HEADS, HD)
    )
    gathered = lax.all_gather((part_max, part_total, part_accum), "ep")
    merged = merge_stack(gathered)
    returned = from_partner(
        (merged[0][row_count:], merged[1][row_count:], merged[2][row_count:]), "grp", 0
    )
    combined = merge_parts(
        (merged[0][:row_count], merged[1][:row_count], merged[2][:row_count]), returned
    )
    own_query = query.reshape(row_count, KV_HEADS, head_group, HD)
    fresh_key = new_kv[:, 0].reshape(row_count, KV_HEADS, HD)
    fresh_value = new_kv[:, 1].astype(jnp.float32).reshape(row_count, KV_HEADS, HD)
    own_score = (
        jnp.einsum(
            "rkgd,rkd->rkg", own_query, fresh_key, preferred_element_type=jnp.float32
        ).reshape(row_count, HEADS)
        * scale
    )
    cache_max, cache_total, cache_accum = combined
    highest = jnp.maximum(cache_max, own_score)
    cache_factor = jnp.exp(cache_max - highest)
    own_weight = jnp.exp(own_score - highest)
    value_rows = jnp.broadcast_to(
        fresh_value[:, :, None, :], (row_count, KV_HEADS, head_group, HD)
    ).reshape(row_count, HEADS, HD)
    numerator = cache_accum * cache_factor[..., None] + own_weight[..., None] * value_rows
    denominator = cache_total * cache_factor + own_weight
    attn_out = (
        (numerator / denominator[..., None]).reshape(row_count, HEADS * HD).astype(jnp.bfloat16)
    )
    weight_columns = lax.all_gather(out_weight, "grp", axis=0, tiled=True)
    projected = jnp.dot(attn_out, weight_columns, preferred_element_type=jnp.float32)
    feature_share = hidden.shape[1]
    mixed = hidden.astype(jnp.float32) + projected
    squares = lax.psum(jnp.sum(mixed * mixed, -1), "ep")
    normed = (mixed * lax.rsqrt(squares / D + norm_epsilon)[:, None] * norm_gain).astype(
        jnp.bfloat16
    )
    capacity = min(row_count, 2 * row_count * TOP // group_count)
    expert_ids = jnp.arange(group_count, dtype=jnp.int32)
    flat_routes = routes.reshape(-1)
    hits = (flat_routes[:, None] == expert_ids[None, :]).astype(jnp.int32)
    earlier_hits = jnp.cumsum(hits, 0) - hits
    position = jnp.sum(earlier_hits * hits, 1)
    slot_index = flat_routes * capacity + position
    slots_all = jnp.arange(group_count * capacity, dtype=jnp.int32)
    picker = jnp.any(
        slot_index.reshape(row_count, TOP)[None, :, :] == slots_all[:, None, None], 2
    ).astype(jnp.bfloat16)
    sender = (
        jnp.dot(picker, normed, preferred_element_type=jnp.float32)
        .astype(jnp.bfloat16)
        .reshape(group_count, capacity, feature_share)
    )
    arrived = lax.all_to_all(sender, "grp", split_axis=0, concat_axis=0, tiled=True)
    whole_rows = lax.all_to_all(
        arrived.reshape(group_count * capacity, feature_share),
        "ep",
        split_axis=0,
        concat_axis=1,
        tiled=True,
    )
    pre_sum = jnp.dot(whole_rows, gate_up[0], preferred_element_type=jnp.float32)
    activated = (jax.nn.silu(pre_sum[:, :FF]) * pre_sum[:, FF:]).astype(jnp.bfloat16)
    result = jnp.dot(activated, down[0], preferred_element_type=jnp.float32).astype(jnp.bfloat16)
    served = lax.all_to_all(result, "ep", split_axis=1, concat_axis=0, tiled=True).reshape(
        group_count, capacity, feature_share
    )
    returned_rows = lax.all_to_all(served, "grp", split_axis=0, concat_axis=0, tiled=True)
    gathered_rows = returned_rows.reshape(group_count * capacity, feature_share)[
        slot_index
    ].reshape(row_count, TOP, feature_share)
    expert_mix = jnp.sum(
        route_weight.astype(jnp.float32)[:, :, None] * gathered_rows.astype(jnp.float32), 1
    )
    layer_out = (mixed + expert_mix).astype(jnp.bfloat16)
    return (layer_out, attn_out)


def solution(mesh):
    placed = (
        P("grp", "ep"),
        P("grp", None),
        P("grp", None, None),
        P(("grp", "ep"), None),
        P(("grp", "ep"), None),
        P(("grp", "ep")),
        P(("grp", "ep")),
        P("grp", "ep"),
        P("ep"),
        P("grp", None, None),
        P("grp", None, None),
        P("grp", None),
        P("grp", None),
    )
    return jax.shard_map(
        per_device,
        mesh=mesh,
        in_specs=placed,
        out_specs=(P("grp", "ep"), P("grp", None)),
        check_vma=False,
    )
```

profile of v0, /device:TPU:1, one launch (start us, length us, event | category | flops | bytes accessed | tf_op | source)
XLA Modules:
  0.0 305.3 jit_solution(13315299732806420359)
XLA Ops:
  7.2 4.2 %collective-permute-start = (bf16[8,1536]{1,0:T(8,128)(2,1)}, bf16[8,1536]{1,0:T(8,128)(2,1)S(1)}, u32[]{:S(2)}, u32[]{:S(2)}) collective-permute-start(bf16[8,1536]{1,0:T(8,128)(2,1)} %param.14), channel_id=1, source_target_pairs={{0,16},{16,0},{32,48},{48,32},{64,80},{80,64},{96,112},{112,96},{1... | collective-permute-start | bytes 73736 | tf_op jit(solution)/shard_map/ppermute | solution.py:23
  13.3 1.8 copy.85
  15.1 1.8 copy.87
  17.8 1.2 select_reduce_fusion
  19.0 1.2 fusion.5
  21.1 1.5 reshape.181
  22.6 1.4 slice_reduce_fusion
  23.9 1.4 reshape.199
  25.3 1.7 fusion.35
  27.0 1.5 copy.105
  28.5 1.3 bitcast_multiply_fusion
  29.8 1.3 mul.132
  31.1 1.4 copy.94
  32.5 1.4 convert_reduce_fusion
  33.8 1.4 reshape.186
  35.2 1.4 copy.96
  36.6 1.3 eq.49
  37.9 1.3 fusion.17
  39.2 1.4 reduce_window_sum.11
  40.6 1.5 select_reduce_fusion.1
  42.1 1.3 reduce_sum.65
  43.4 1.3 broadcast_multiply_fusion
  45.4 61.6 %all_gather.15 = bf16[1536,96]{1,0:T(8,128)(2,1)} all-gather(bf16[48,96]{1,0:T(8,128)(2,1)} %param.20), channel_id=1, replica_groups=mesh['grp'=32,'ep'=16] {'grp'}, dimensions={0}, use_global_device_ids=true | all-gather | bytes 304128 | tf_op jit(solution)/shard_map/all_gather | solution.py:143
  108.5 1.4 copy.98
  109.9 1.3 reduce_sum.62
  112.7 1.4 copy.100
  114.1 1.3 reduce_max.21
  117.6 40.9 %all_gather.13 = f32[16,16,24]{2,1,0:T(8,128)} all-gather(f32[1,16,24]{2,1,0:T(8,128)S(1)} %copy.93), channel_id=1, replica_groups=mesh['grp'=32,'ep'=16] {'ep'}, dimensions={0}, use_global_device_ids=true | all-gather | bytes 26112 | tf_op jit(solution)/shard_map/all_gather | solution.py:114
  158.6 0.9 reduce_max.22
  160.1 20.0 %all_gather.14 = f32[16,16,24]{2,1,0:T(8,128)S(1)} all-gather(f32[1,16,24]{2,1,0:T(8,128)} %copy.100), channel_id=1, replica_groups=mesh['grp'=32,'ep'=16] {'ep'}, dimensions={0}, use_global_device_ids=true | all-gather | bytes 26112 | tf_op jit(solution)/shard_map/all_gather | solution.py:114
  180.1 1.6 multiply_reduce_fusion.1
  182.3 1.9 collective-permute-start.3
  184.2 3.4 %collective-permute-start.1 = (f32[8,24]{1,0:T(8,128)}, f32[8,24]{1,0:T(8,128)}, u32[]{:S(2)}, u32[]{:S(2)}) collective-permute-start(f32[8,24]{1,0:T(8,128)} %slice.44), channel_id=1, source_target_pairs={{0,16},{16,0},{32,48},{48,32},{64,80},{80,64},{96,112},{112,96},{1... | collective-permute-start | bytes 2312 | tf_op jit(solution)/shard_map/ppermute | solution.py:23
  187.6 2.4 multiply_reduce_fusion
  190.0 1.9 collective-permute-start.2
  192.7 2.7 collective-permute-done.2
  196.3 1.5 convert_element_type.56
  197.8 1.0 multiply_reduce_fusion.2
  198.8 34.4 %psum.7 = f32[8]{0:T(128)S(1)} all-reduce(f32[8]{0:T(128)S(1)} %get-tuple-element.13), channel_id=1, replica_groups=mesh['grp'=32,'ep'=16] {'ep'}, use_global_device_ids=true, to_apply=%region_9.10 | all-reduce | flops 8 | bytes 64 | tf_op jit(solution)/shard_map/psum | solution.py:147
  233.2 1.0 convolution_convert_fusion.1
  234.3 18.4 %all_to_all.45 = bf16[32,4,96]{2,1,0:T(4,128)(2,1)} all-to-all(bf16[32,4,96]{2,1,0:T(4,128)(2,1)S(1)} %bitcast.63), channel_id=1, replica_groups=mesh['grp'=32,'ep'=16] {'grp'}, dimensions={0} | all-to-all | bytes 49152 | tf_op jit(solution)/shard_map/all_to_all | solution.py:167
  252.7 6.8 %all-to-all-start.1 = ((bf16[16,8,96]{2,1,0:T(8,128)(2,1)}), bf16[16,8,96]{2,1,0:T(8,128)(2,1)S(1)}, u32[]{:S(2)}, u32[]{:S(2)}) async-start(bf16[16,8,96]{2,1,0:T(8,128)(2,1)} %bitcast.12), calls=%async_computation.1 | async-start | bytes 65536 | tf_op jit(solution)/shard_map/all_to_all | solution.py:168
  260.2 6.6 %all-to-all-done.1 = bf16[16,8,96]{2,1,0:T(8,128)(2,1)S(1)} async-done(((bf16[16,8,96]{2,1,0:T(8,128)(2,1)}), bf16[16,8,96]{2,1,0:T(8,128)(2,1)S(1)}, u32[]{:S(2)}, u32[]{:S(2)}) %all-to-all-start.1) | async-done | bytes 24608 | tf_op jit(solution)/shard_map/all_to_all | solution.py:168
  267.4 0.9 copy-done.1
  269.4 4.2 %all-to-all-start.2 = ((bf16[8,16,96]{2,0,1:T(8,128)(2,1)}), bf16[8,16,96]{2,0,1:T(8,128)(2,1)}, u32[]{:S(2)}, u32[]{:S(2)}) async-start(bf16[8,16,96]{2,0,1:T(8,128)(2,1)} %copy.103), calls=%async_computation.2 | async-start | bytes 65536 | tf_op jit(solution)/shard_map/all_to_all | solution.py:178
  273.6 7.4 %all-to-all-done.2 = bf16[8,16,96]{2,0,1:T(8,128)(2,1)} async-done(((bf16[8,16,96]{2,0,1:T(8,128)(2,1)}), bf16[8,16,96]{2,0,1:T(8,128)(2,1)}, u32[]{:S(2)}, u32[]{:S(2)}) %all-to-all-start.2) | async-done | bytes 24608 | tf_op jit(solution)/shard_map/all_to_all | solution.py:178
  281.1 3.9 %all-to-all-start.3 = ((bf16[32,4,96]{2,1,0:T(4,128)(2,1)}), bf16[32,4,96]{2,1,0:T(4,128)(2,1)S(1)}, u32[]{:S(2)}, u32[]{:S(2)}) async-start(bf16[32,4,96]{2,1,0:T(4,128)(2,1)} %bitcast.17), calls=%async_computation.3 | async-start | bytes 65536 | tf_op jit(solution)/shard_map/all_to_all | solution.py:181
  284.9 12.2 %all-to-all-done.3 = bf16[32,4,96]{2,1,0:T(4,128)(2,1)S(1)} async-done(((bf16[32,4,96]{2,1,0:T(4,128)(2,1)}), bf16[32,4,96]{2,1,0:T(4,128)(2,1)S(1)}, u32[]{:S(2)}, u32[]{:S(2)}) %all-to-all-start.3) | async-done | bytes 24608 | tf_op jit(solution)/shard_map/all_to_all | solution.py:181
  (65 shorter events, 16.1 us)
Async XLA Ops:
  7.2 259.7 %copy-start = (bf16[1,1536,1024]{2,1,0:T(8,128)(2,1)S(1)}, bf16[1,1536,1024]{2,1,0:T(8,128)(2,1)}, u32[]{:S(2)}) copy-start(bf16[1,1536,1024]{2,1,0:T(8,128)(2,1)} %param.22) | copy-start | bytes 9437188
  7.2 180.4 %all-gather.2.cloned.1.call-start = ((), (), s32[]{:S(2)}) async-start(), calls=%async_computation.4 | async-start | bytes 3342336 | tf_op jit(solution)/shard_map/all_gather | solution.py:114
  7.2 9.6 %collective-permute-start = (bf16[8,1536]{1,0:T(8,128)(2,1)}, bf16[8,1536]{1,0:T(8,128)(2,1)S(1)}, u32[]{:S(2)}, u32[]{:S(2)}) collective-permute-start(bf16[8,1536]{1,0:T(8,128)(2,1)} %param.14), channel_id=1, source_target_pairs={{0,16},{16,0},{32,48},{48,32},{64,80},{80,64},{96,112},{112,96},{1... | collective-permute-start | bytes 73736 | tf_op jit(solution)/shard_map/ppermute | solution.py:23
  108.5 89.3 %copy-start.2 = (bf16[1536,96]{1,0:T(8,128)(2,1)S(1)}, bf16[1536,96]{1,0:T(8,128)(2,1)}, u32[]{:S(2)}) copy-start(bf16[1536,96]{1,0:T(8,128)(2,1)} %all_gather.15) | copy-start | bytes 884740
  182.3 9.7 %collective-permute-start.3 = (f32[8,24]{1,0:T(8,128)}, f32[8,24]{1,0:T(8,128)}, u32[]{:S(2)}, u32[]{:S(2)}) collective-permute-start(f32[8,24]{1,0:T(8,128)} %slice.47), channel_id=1, source_target_pairs={{0,16},{16,0},{32,48},{48,32},{64,80},{80,64},{96,112},{112,96},{1... | collective-permute-start | bytes 2312 | tf_op jit(solution)/shard_map/ppermute | solution.py:23
  184.2 7.8 %collective-permute-start.1 = (f32[8,24]{1,0:T(8,128)}, f32[8,24]{1,0:T(8,128)}, u32[]{:S(2)}, u32[]{:S(2)}) collective-permute-start(f32[8,24]{1,0:T(8,128)} %slice.44), channel_id=1, source_target_pairs={{0,16},{16,0},{32,48},{48,32},{64,80},{80,64},{96,112},{112,96},{1... | collective-permute-start | bytes 2312 | tf_op jit(solution)/shard_map/ppermute | solution.py:23
  187.6 4.4 %copy-start.4 = (f32[8,24]{1,0:T(8,128)S(1)}, f32[8,24]{1,0:T(8,128)}, u32[]{:S(2)}) copy-start(f32[8,24]{1,0:T(8,128)} %copy.94) | copy-start | bytes 2308
  187.6 7.8 %copy-start.3 = (f32[8,8,64]{2,0,1:T(8,128)S(1)}, f32[8,8,64]{2,0,1:T(8,128)}, u32[]{:S(2)}) copy-start(f32[8,8,64]{2,0,1:T(8,128)} %copy.96) | copy-start | bytes 49156
  190.0 5.4 %collective-permute-start.2 = (f32[8,24,64]{2,1,0:T(8,128)S(1)}, f32[8,24,64]{2,1,0:T(8,128)S(1)}, u32[]{:S(2)}, u32[]{:S(2)}) collective-permute-start(f32[8,24,64]{2,1,0:T(8,128)S(1)} %slice.45), channel_id=1, source_target_pairs={{0,16},{16,0},{32,48},{48,32},{64,80},{80,64},{96,112},{112,96},{1... | collective-permute-start | bytes 147464 | tf_op jit(solution)/shard_map/ppermute | solution.py:23
  195.4 78.2 %copy-start.5 = (s32[64]{0:T(128)S(1)}, s32[64]{0:T(128)}, u32[]{:S(2)}) copy-start(s32[64]{0:T(128)} %select_reduce_fusion.1) | copy-start | bytes 772
  195.4 78.2 %copy-start.6 = (bf16[8,8]{1,0:T(8,128)(2,1)S(1)}, bf16[8,8]{1,0:T(8,128)(2,1)}, u32[]{:S(2)}) copy-start(bf16[8,8]{1,0:T(8,128)(2,1)} %param.25) | copy-start | bytes 388
  252.7 14.1 %all-to-all-start.1 = ((bf16[16,8,96]{2,1,0:T(8,128)(2,1)}), bf16[16,8,96]{2,1,0:T(8,128)(2,1)S(1)}, u32[]{:S(2)}, u32[]{:S(2)}) async-start(bf16[16,8,96]{2,1,0:T(8,128)(2,1)} %bitcast.12), calls=%async_computation.1 | async-start | bytes 65536 | tf_op jit(solution)/shard_map/all_to_all | solution.py:168
  266.9 1.4 copy-start.1
  269.4 11.7 %all-to-all-start.2 = ((bf16[8,16,96]{2,0,1:T(8,128)(2,1)}), bf16[8,16,96]{2,0,1:T(8,128)(2,1)}, u32[]{:S(2)}, u32[]{:S(2)}) async-start(bf16[8,16,96]{2,0,1:T(8,128)(2,1)} %copy.103), calls=%async_computation.2 | async-start | bytes 65536 | tf_op jit(solution)/shard_map/all_to_all | solution.py:178
  281.1 16.1 %all-to-all-start.3 = ((bf16[32,4,96]{2,1,0:T(4,128)(2,1)}), bf16[32,4,96]{2,1,0:T(4,128)(2,1)S(1)}, u32[]{:S(2)}, u32[]{:S(2)}) async-start(bf16[32,4,96]{2,1,0:T(4,128)(2,1)} %bitcast.17), calls=%async_computation.3 | async-start | bytes 65536 | tf_op jit(solution)/shard_map/all_to_all | solution.py:181
Sparse Core Ops, SparseCore 0:
  21.2 72.1 all-gather.1
where the time goes:
time: 307 us; the launch traced here: 305 us
  blocking collectives  175 us (57%)
  local copies, waits for them, and re-layouts  35.2 us (11%)
  waiting for transfers between devices  29 us (9%)
  starting transfers between devices  26.3 us (9%)
  other arithmetic  18.3 us (6%)
  between operations  14.3 us (5%)
  matrix products  6.86 us (2%)
    all_gather x1, blocking collectives, per_device(): weight_columns = lax.all_gather(out_weight, 'grp', axis=0, tiled=True)  61.6 us
    all_gather x2, blocking collectives, per_device(): gathered = lax.all_gather((part_max, part_total, part_accum), 'ep')  60.9 us
    psum x1, blocking collectives, per_device(): squares = lax.psum(jnp.sum(mixed * mixed, -1), 'ep')  34.4 us
    all_to_all x1, blocking collectives, per_device(): lax.all_to_all(sender, 'grp', split_axis=0, concat_axis=0, tiled=True)  18.4 us
    all_to_all x1, waiting for transfers between devices, per_device(): lax.all_to_all(served, 'grp', split_axis=0, concat_axis=0, tiled=True)  12.2 us
    ppermute x4, starting transfers between devices, from_partner(): return lax.ppermute(block, axis, route)  11.4 us
    all_to_all x1, waiting for transfers between devices, per_device(): lax.all_to_all(result, 'ep', split_axis=1, concat_axis=0, tiled=True)  7.43 us
    all_to_all x1, starting transfers between devices, per_device(): lax.all_to_all(arrived.reshape(group_count * capacity, feature_share), 'e...  6.75 us
  transfers between devices with their start and end apart: 8, of which 4 were waited for; matrix products, arithmetic and copies ran while one was open for 16% of the time, Pallas kernels for 0%

commit v1 on v0

--- a/solution.py
+++ b/solution.py
@@ -165,12 +165,20 @@
         .reshape(group_count, capacity, feature_share)
     )
     arrived = lax.all_to_all(sender, "grp", split_axis=0, concat_axis=0, tiled=True)
-    whole_rows = lax.all_to_all(
-        arrived.reshape(group_count * capacity, feature_share),
-        "ep",
-        split_axis=0,
-        concat_axis=1,
-        tiled=True,
+    whole_rows = jnp.concatenate(
+        lax.all_to_all(
+            jnp.stack(
+                jnp.split(
+                    arrived.reshape(group_count * capacity, feature_share),
+                    lax.axis_size("ep"),
+                    axis=0,
+                )
+            ),
+            "ep",
+            0,
+            0,
+        ),
+        axis=1,
     )
     pre_sum = jnp.dot(whole_rows, gate_up[0], preferred_element_type=jnp.float32)
     activated = (jax.nn.silu(pre_sum[:, :FF]) * pre_sum[:, FF:]).astype(jnp.bfloat16)

time: 307 us -> 317 us (1.033)
  local copies, waits for them, and re-layouts: 35.2 us -> 44.6 us
    unnamed x16 -> x31, local copies, waits for them, and re-layouts: 4.44 us -> 13.2 us
  transfers between devices with their start and end apart: 8 -> 8, of which waited for: 4 -> 4; matrix products, arithmetic and copies ran while one was open for 16% -> 15% of each run, Pallas kernels for 0% -> 0%
where the time goes in v1:
time: 317 us; the launch traced here: 315 us
  blocking collectives  175 us (55%)
  local copies, waits for them, and re-layouts  44.6 us (14%)
  waiting for transfers between devices  29 us (9%)
  starting transfers between devices  26.3 us (8%)
  other arithmetic  18.3 us (6%)
  between operations  14.3 us (5%)
  matrix products  6.86 us (2%)
    all_gather x1, blocking collectives, per_device(): weight_columns = lax.all_gather(out_weight, 'grp', axis=0, tiled=True)  61.6 us
    all_gather x2, blocking collectives, per_device(): gathered = lax.all_gather((part_max, part_total, part_accum), 'ep')  60.9 us
    psum x1, blocking collectives, per_device(): squares = lax.psum(jnp.sum(mixed * mixed, -1), 'ep')  34.4 us
    all_to_all x1, blocking collectives, per_device(): lax.all_to_all(sender, 'grp', split_axis=0, concat_axis=0, tiled=True)  18.3 us
    unnamed x31, local copies, waits for them, and re-layouts  13.2 us
    all_to_all x1, waiting for transfers between devices, per_device(): lax.all_to_all(served, 'grp', split_axis=0, concat_axis=0, tiled=True)  12.2 us
    ppermute x4, starting transfers between devices, from_partner(): return lax.ppermute(block, axis, route)  11.4 us
    all_to_all x1, waiting for transfers between devices, per_device(): lax.all_to_all(result, 'ep', split_axis=1, concat_axis=0, tiled=True)  7.43 us
  transfers between devices with their start and end apart: 8, of which 4 were waited for; matrix products, arithmetic and copies ran while one was open for 15% of the time, Pallas kernels for 0%

profile of v1, /device:TPU:1, one launch (start us, length us, event | category | flops | bytes accessed | tf_op | source)
XLA Modules:
  0.0 314.5 jit_solution(641656666454987090)
XLA Ops:
  7.2 4.2 %collective-permute-start = (bf16[8,1536]{1,0:T(8,128)(2,1)}, bf16[8,1536]{1,0:T(8,128)(2,1)S(1)}, u32[]{:S(2)}, u32[]{:S(2)}) collective-permute-start(bf16[8,1536]{1,0:T(8,128)(2,1)} %param.14), channel_id=1, source_target_pairs={{0,16},{16,0},{32,48},{48,32},{64,80},{80,64},{96,112},{112,96},{1... | collective-permute-start | bytes 73736 | tf_op jit(solution)/shard_map/ppermute | solution.py:23
  13.3 1.8 copy.84
  15.1 1.8 copy.86
  17.8 1.2 select_reduce_fusion
  19.0 1.2 fusion.5
  21.1 1.5 reshape.215
  22.6 1.4 slice_reduce_fusion
  23.9 1.4 reshape.235
  25.3 1.7 fusion.36
  27.0 1.5 copy.104
  28.5 1.3 bitcast_multiply_fusion
  29.8 1.3 mul.132
  31.1 1.4 copy.93
  32.5 1.4 convert_reduce_fusion
  33.8 1.4 reshape.222
  35.2 1.4 copy.95
  36.6 1.3 eq.49
  37.9 1.3 fusion.17
  39.2 1.4 reduce_window_sum.11
  40.6 1.5 select_reduce_fusion.1
  42.1 1.3 reduce_sum.65
  43.4 1.3 broadcast_multiply_fusion
  45.4 61.6 %all_gather.15 = bf16[1536,96]{1,0:T(8,128)(2,1)} all-gather(bf16[48,96]{1,0:T(8,128)(2,1)} %param.20), channel_id=1, replica_groups=mesh['grp'=32,'ep'=16] {'grp'}, dimensions={0}, use_global_device_ids=true | all-gather | bytes 304128 | tf_op jit(solution)/shard_map/all_gather | solution.py:143
  108.5 1.4 copy.97
  109.9 1.3 reduce_sum.62
  112.7 1.4 copy.99
  114.1 1.3 reduce_max.21
  117.6 40.9 %all_gather.13 = f32[16,16,24]{2,1,0:T(8,128)} all-gather(f32[1,16,24]{2,1,0:T(8,128)S(1)} %copy.92), channel_id=1, replica_groups=mesh['grp'=32,'ep'=16] {'ep'}, dimensions={0}, use_global_device_ids=true | all-gather | bytes 26112 | tf_op jit(solution)/shard_map/all_gather | solution.py:114
  158.6 0.9 reduce_max.22
  160.1 20.0 %all_gather.14 = f32[16,16,24]{2,1,0:T(8,128)S(1)} all-gather(f32[1,16,24]{2,1,0:T(8,128)} %copy.99), channel_id=1, replica_groups=mesh['grp'=32,'ep'=16] {'ep'}, dimensions={0}, use_global_device_ids=true | all-gather | bytes 26112 | tf_op jit(solution)/shard_map/all_gather | solution.py:114
  180.1 1.6 multiply_reduce_fusion.1
  182.3 1.9 collective-permute-start.3
  184.2 3.4 %collective-permute-start.1 = (f32[8,24]{1,0:T(8,128)}, f32[8,24]{1,0:T(8,128)}, u32[]{:S(2)}, u32[]{:S(2)}) collective-permute-start(f32[8,24]{1,0:T(8,128)} %slice.60), channel_id=1, source_target_pairs={{0,16},{16,0},{32,48},{48,32},{64,80},{80,64},{96,112},{112,96},{1... | collective-permute-start | bytes 2312 | tf_op jit(solution)/shard_map/ppermute | solution.py:23
  187.6 2.4 multiply_reduce_fusion
  190.0 1.9 collective-permute-start.2
  192.7 2.7 collective-permute-done.2
  196.2 1.5 convert_element_type.56
  197.8 1.0 multiply_reduce_fusion.2
  198.8 34.4 %psum.7 = f32[8]{0:T(128)S(1)} all-reduce(f32[8]{0:T(128)S(1)} %get-tuple-element.29), channel_id=1, replica_groups=mesh['grp'=32,'ep'=16] {'ep'}, use_global_device_ids=true, to_apply=%region_9.10 | all-reduce | flops 8 | bytes 64 | tf_op jit(solution)/shard_map/psum | solution.py:147
  233.2 1.0 convolution_convert_fusion.1
  234.3 18.3 %all_to_all.31 = bf16[32,4,96]{2,1,0:T(4,128)(2,1)S(1)} all-to-all(bf16[32,4,96]{2,1,0:T(4,128)(2,1)S(1)} %bitcast.110), channel_id=1, replica_groups=mesh['grp'=32,'ep'=16] {'grp'}, dimensions={0} | all-to-all | bytes 49152 | tf_op jit(solution)/shard_map/all_to_all | solution.py:167
  261.9 6.8 %all-to-all-start.1 = ((bf16[16,8,96]{2,1,0:T(8,128)(2,1)}), bf16[16,8,96]{2,1,0:T(8,128)(2,1)S(1)}, u32[]{:S(2)}, u32[]{:S(2)}) async-start(bf16[16,8,96]{2,1,0:T(8,128)(2,1)} %constant_dynamic-update-slice_fusion), calls=%async_computation.1 | async-start | bytes 65536 | tf_op jit(solution)/shard_map/all_to_all | solution.py:169
  269.4 6.6 %all-to-all-done.1 = bf16[16,8,96]{2,1,0:T(8,128)(2,1)S(1)} async-done(((bf16[16,8,96]{2,1,0:T(8,128)(2,1)}), bf16[16,8,96]{2,1,0:T(8,128)(2,1)S(1)}, u32[]{:S(2)}, u32[]{:S(2)}) %all-to-all-start.1) | async-done | bytes 24608 | tf_op jit(solution)/shard_map/all_to_all | solution.py:169
  276.7 0.9 copy-done.1
  278.6 4.2 %all-to-all-start.2 = ((bf16[8,16,96]{2,0,1:T(8,128)(2,1)}), bf16[8,16,96]{2,0,1:T(8,128)(2,1)}, u32[]{:S(2)}, u32[]{:S(2)}) async-start(bf16[8,16,96]{2,0,1:T(8,128)(2,1)} %copy.102), calls=%async_computation.2 | async-start | bytes 65536 | tf_op jit(solution)/shard_map/all_to_all | solution.py:186
  282.9 7.4 %all-to-all-done.2 = bf16[8,16,96]{2,0,1:T(8,128)(2,1)} async-done(((bf16[8,16,96]{2,0,1:T(8,128)(2,1)}), bf16[8,16,96]{2,0,1:T(8,128)(2,1)}, u32[]{:S(2)}, u32[]{:S(2)}) %all-to-all-start.2) | async-done | bytes 24608 | tf_op jit(solution)/shard_map/all_to_all | solution.py:186
  290.3 3.9 %all-to-all-start.3 = ((bf16[32,4,96]{2,1,0:T(4,128)(2,1)}), bf16[32,4,96]{2,1,0:T(4,128)(2,1)S(1)}, u32[]{:S(2)}, u32[]{:S(2)}) async-start(bf16[32,4,96]{2,1,0:T(4,128)(2,1)} %bitcast.32), calls=%async_computation.3 | async-start | bytes 65536 | tf_op jit(solution)/shard_map/all_to_all | solution.py:189
  294.2 12.2 %all-to-all-done.3 = bf16[32,4,96]{2,1,0:T(4,128)(2,1)S(1)} async-done(((bf16[32,4,96]{2,1,0:T(4,128)(2,1)}), bf16[32,4,96]{2,1,0:T(4,128)(2,1)S(1)}, u32[]{:S(2)}, u32[]{:S(2)}) %all-to-all-start.3) | async-done | bytes 24608 | tf_op jit(solution)/shard_map/all_to_all | solution.py:189
  (82 shorter events, 25.5 us)
Async XLA Ops:
  7.2 269.0 %copy-start = (bf16[1,1536,1024]{2,1,0:T(8,128)(2,1)S(1)}, bf16[1,1536,1024]{2,1,0:T(8,128)(2,1)}, u32[]{:S(2)}) copy-start(bf16[1,1536,1024]{2,1,0:T(8,128)(2,1)} %param.22) | copy-start | bytes 9437188
  7.2 180.4 %all-gather.2.cloned.1.call-start = ((), (), s32[]{:S(2)}) async-start(), calls=%async_computation.4 | async-start | bytes 3342336 | tf_op jit(solution)/shard_map/all_gather | solution.py:114
  7.2 9.6 %collective-permute-start = (bf16[8,1536]{1,0:T(8,128)(2,1)}, bf16[8,1536]{1,0:T(8,128)(2,1)S(1)}, u32[]{:S(2)}, u32[]{:S(2)}) collective-permute-start(bf16[8,1536]{1,0:T(8,128)(2,1)} %param.14), channel_id=1, source_target_pairs={{0,16},{16,0},{32,48},{48,32},{64,80},{80,64},{96,112},{112,96},{1... | collective-permute-start | bytes 73736 | tf_op jit(solution)/shard_map/ppermute | solution.py:23
  108.5 89.3 %copy-start.2 = (bf16[1536,96]{1,0:T(8,128)(2,1)S(1)}, bf16[1536,96]{1,0:T(8,128)(2,1)}, u32[]{:S(2)}) copy-start(bf16[1536,96]{1,0:T(8,128)(2,1)} %all_gather.15) | copy-start | bytes 884740
  182.3 9.7 %collective-permute-start.3 = (f32[8,24]{1,0:T(8,128)}, f32[8,24]{1,0:T(8,128)}, u32[]{:S(2)}, u32[]{:S(2)}) collective-permute-start(f32[8,24]{1,0:T(8,128)} %slice.63), channel_id=1, source_target_pairs={{0,16},{16,0},{32,48},{48,32},{64,80},{80,64},{96,112},{112,96},{1... | collective-permute-start | bytes 2312 | tf_op jit(solution)/shard_map/ppermute | solution.py:23
  184.2 7.8 %collective-permute-start.1 = (f32[8,24]{1,0:T(8,128)}, f32[8,24]{1,0:T(8,128)}, u32[]{:S(2)}, u32[]{:S(2)}) collective-permute-start(f32[8,24]{1,0:T(8,128)} %slice.60), channel_id=1, source_target_pairs={{0,16},{16,0},{32,48},{48,32},{64,80},{80,64},{96,112},{112,96},{1... | collective-permute-start | bytes 2312 | tf_op jit(solution)/shard_map/ppermute | solution.py:23
  187.6 4.4 %copy-start.4 = (f32[8,24]{1,0:T(8,128)S(1)}, f32[8,24]{1,0:T(8,128)}, u32[]{:S(2)}) copy-start(f32[8,24]{1,0:T(8,128)} %copy.93) | copy-start | bytes 2308
  187.6 7.8 %copy-start.3 = (f32[8,8,64]{2,0,1:T(8,128)S(1)}, f32[8,8,64]{2,0,1:T(8,128)}, u32[]{:S(2)}) copy-start(f32[8,8,64]{2,0,1:T(8,128)} %copy.95) | copy-start | bytes 49156
  190.0 5.4 %collective-permute-start.2 = (f32[8,24,64]{2,1,0:T(8,128)S(1)}, f32[8,24,64]{2,1,0:T(8,128)S(1)}, u32[]{:S(2)}, u32[]{:S(2)}) collective-permute-start(f32[8,24,64]{2,1,0:T(8,128)S(1)} %slice.61), channel_id=1, source_target_pairs={{0,16},{16,0},{32,48},{48,32},{64,80},{80,64},{96,112},{112,96},{1... | collective-permute-start | bytes 147464 | tf_op jit(solution)/shard_map/ppermute | solution.py:23
  196.2 86.6 %copy-start.5 = (s32[64]{0:T(128)S(1)}, s32[64]{0:T(128)}, u32[]{:S(2)}) copy-start(s32[64]{0:T(128)} %select_reduce_fusion.1) | copy-start | bytes 772
  196.2 86.6 %copy-start.6 = (bf16[8,8]{1,0:T(8,128)(2,1)S(1)}, bf16[8,8]{1,0:T(8,128)(2,1)}, u32[]{:S(2)}) copy-start(bf16[8,8]{1,0:T(8,128)(2,1)} %param.25) | copy-start | bytes 388
  261.9 14.1 %all-to-all-start.1 = ((bf16[16,8,96]{2,1,0:T(8,128)(2,1)}), bf16[16,8,96]{2,1,0:T(8,128)(2,1)S(1)}, u32[]{:S(2)}, u32[]{:S(2)}) async-start(bf16[16,8,96]{2,1,0:T(8,128)(2,1)} %constant_dynamic-update-slice_fusion), calls=%async_computation.1 | async-start | bytes 65536 | tf_op jit(solution)/shard_map/all_to_all | solution.py:169
  276.1 1.4 copy-start.1
  278.6 11.7 %all-to-all-start.2 = ((bf16[8,16,96]{2,0,1:T(8,128)(2,1)}), bf16[8,16,96]{2,0,1:T(8,128)(2,1)}, u32[]{:S(2)}, u32[]{:S(2)}) async-start(bf16[8,16,96]{2,0,1:T(8,128)(2,1)} %copy.102), calls=%async_computation.2 | async-start | bytes 65536 | tf_op jit(solution)/shard_map/all_to_all | solution.py:186
  290.3 16.1 %all-to-all-start.3 = ((bf16[32,4,96]{2,1,0:T(4,128)(2,1)}), bf16[32,4,96]{2,1,0:T(4,128)(2,1)S(1)}, u32[]{:S(2)}, u32[]{:S(2)}) async-start(bf16[32,4,96]{2,1,0:T(4,128)(2,1)} %bitcast.32), calls=%async_computation.3 | async-start | bytes 65536 | tf_op jit(solution)/shard_map/all_to_all | solution.py:189
Sparse Core Ops, SparseCore 0:
  21.2 72.1 all-gather.1
